TPU v7x, 512 devices: a whole 4x8x8 slice. The times are simulated.
512 devices in a mesh: wide: 64 (over x, y, core), chain: 8 (over z).
Axes of the slice: x: 4, y: 8, z: 8, core: 2. Of those that a mesh axis runs over, the one named last changes fastest.
Arguments:
- queries: bfloat16 [131072, 1024], P(('chain', 'wide')), may hold values from -4 to 4
- keys: bfloat16 [131072, 1024], P(('chain', 'wide')), may hold values from -4 to 4
- values: bfloat16 [131072, 1024], P(('chain', 'wide')), may hold values from -6 to 6
Outputs:
- attended: bfloat16 [131072, 1024], P(('chain', 'wide'))
All inputs are finite; a program needn't handle non-finite values.
Results may differ from a plain program's by a relative error of at most 0.005.
Values may be sent and summed in bfloat16 or wider, within the bound.
A program may use at most 64 MiB of HBM per device.

v0:
```python
import jax
import jax.numpy as jnp
from jax import lax
from jax.sharding import PartitionSpec as P

HEADS = 16
HEAD_DIM = 64


def carried_in(x, axis, combine, identity):
    peers, index = (lax.axis_size(axis), lax.axis_index(axis))
    everything = lax.all_gather(x, axis)
    start = jnp.broadcast_to(jnp.asarray(identity, x.dtype), x.shape)

    def step(k, before):
        reached = k < index
        new = combine(before, everything[k])
        return jnp.where(reached, new, before)

    return lax.fori_loop(0, peers, step, start)


def spread(block, axis, source):
    block = jnp.where(lax.axis_index(axis) == source, block, jnp.zeros_like(block))
    return lax.psum(block, axis)


def add_states(earlier, later):
    return earlier + later


def per_device(queries, keys, values):
    rows = queries.shape[0]
    q_blk = queries.reshape(rows, HEADS, HEAD_DIM)
    k_blk = keys.reshape(rows, HEADS, HEAD_DIM)
    v_blk = values.reshape(rows, HEADS, HEAD_DIM)
    states = jnp.einsum("the,thf->hef", k_blk, v_blk, preferred_element_type=jnp.float32)
    flat_states = states.reshape(HEADS, HEAD_DIM * HEAD_DIM)
    zeros = jnp.zeros_like(flat_states)
    inner = carried_in(flat_states, "wide", add_states, zeros)
    group = spread(inner + flat_states, "wide", lax.axis_size("wide") - 1)
    outer = carried_in(group, "chain", add_states, zeros)
    prefix = (outer + inner).astype(jnp.bfloat16).reshape(HEADS, HEAD_DIM, HEAD_DIM)
    inter = jnp.einsum("the,hef->thf", q_blk, prefix, preferred_element_type=jnp.float32)
    causal = jnp.arange(rows)[:, None] >= jnp.arange(rows)[None, :]
    scores = jnp.einsum("the,she->hts", q_blk, k_blk, preferred_element_type=jnp.float32)
    scores = jnp.where(causal[None], scores, 0.0).astype(jnp.bfloat16)
    intra = jnp.einsum("hts,shf->thf", scores, v_blk, preferred_element_type=jnp.float32)
    total = intra + inter
    normed = total / jnp.sqrt(jnp.mean(total * total, axis=-1, keepdims=True) + 1e-06)
    return normed.astype(jnp.bfloat16).reshape(rows, HEADS * HEAD_DIM)


def solution(mesh):
    placed = (P(("chain", "wide"), None), P(("chain", "wide"), None), P(("chain", "wide"), None))
    return jax.shard_map(
        per_device,
        mesh=mesh,
        in_specs=placed,
        out_specs=P(("chain", "wide"), None),
        check_vma=False,
    )
```

profile of v0, /device:TPU:2, one launch (start us, length us, event | category | flops | bytes accessed | tf_op | source)
XLA Modules:
  0.0 433.9 jit_solution(11462673946460893660)
XLA Ops:
  6.5 1.2 copy.16
  7.8 1.2 copy.17
  10.5 108.4 %all-gather.3.cloned.1.call-done = f32[64,16,4096]{2,1,0:T(8,128)} async-done(((f32[1,16,4096]{2,1,0:T(8,128)}), f32[64,16,4096]{2,1,0:T(8,128)}) %all-gather.3.cloned.1.call-update) | async-done | bytes 16777232 | tf_op jit(solution)/shard_map/all_gather | solution.py:12
  118.9 67.6 %while.28 = (s32[]{:T(128)}, f32[16,4096]{1,0:T(8,128)S(1)}, s32[]{:T(128)}, f32[64,16,4096]{2,1,0:T(8,128)}, s32[]{:T(128)}, /*index=5*/s32[]{:T(128)}) while((s32[]{:T(128)}, f32[16,4096]{1,0:T(8,128)S(1)}, s32[]{:T(128)}, f32[64,16,4096]{2,1,0:T(8,128)}, s32[]{:T(128)}, /*index=5*/s32[]{:T(128)}) %tuple.60), condition=%wide.region_1.2_spmd.clone, body=%wide.region_0.1_spmd.clone.sunk | while | flops 196612 | bytes 786525 | solution.py:20
  120.0 1.0 add_select_fusion.4
  121.1 1.0 add_select_fusion.4
  122.1 1.0 add_select_fusion.4
  123.2 1.0 add_select_fusion.4
  124.2 1.0 add_select_fusion.4
  125.3 1.0 add_select_fusion.4
  126.3 1.0 add_select_fusion.4
  127.4 1.0 add_select_fusion.4
  128.5 1.0 add_select_fusion.4
  129.5 1.0 add_select_fusion.4
  130.6 1.0 add_select_fusion.4
  131.6 1.0 add_select_fusion.4
  132.7 1.0 add_select_fusion.4
  133.7 1.0 add_select_fusion.4
  134.8 1.0 add_select_fusion.4
  135.9 1.0 add_select_fusion.4
  136.9 1.0 add_select_fusion.4
  138.0 1.0 add_select_fusion.4
  139.0 1.0 add_select_fusion.4
  140.1 1.0 add_select_fusion.4
  141.1 1.0 add_select_fusion.4
  142.2 1.0 add_select_fusion.4
  143.3 1.0 add_select_fusion.4
  144.3 1.0 add_select_fusion.4
  145.4 1.0 add_select_fusion.4
  146.4 1.0 add_select_fusion.4
  147.5 1.0 add_select_fusion.4
  148.5 1.0 add_select_fusion.4
  149.6 1.0 add_select_fusion.4
  150.7 1.0 add_select_fusion.4
  151.7 1.0 add_select_fusion.4
  152.8 1.0 add_select_fusion.4
  153.8 1.0 add_select_fusion.4
  154.9 1.0 add_select_fusion.4
  155.9 1.0 add_select_fusion.4
  157.0 1.0 add_select_fusion.4
  158.1 1.0 add_select_fusion.4
  159.1 1.0 add_select_fusion.4
  160.2 1.0 add_select_fusion.4
  161.2 1.0 add_select_fusion.4
  162.3 1.0 add_select_fusion.4
  163.3 1.0 add_select_fusion.4
  164.4 1.0 add_select_fusion.4
  165.5 1.0 add_select_fusion.4
  166.5 1.0 add_select_fusion.4
  167.6 1.0 add_select_fusion.4
  168.6 1.0 add_select_fusion.4
  169.7 1.0 add_select_fusion.4
  170.7 1.0 add_select_fusion.4
  171.8 1.0 add_select_fusion.4
  172.9 1.0 add_select_fusion.4
  173.9 1.0 add_select_fusion.4
  175.0 1.0 add_select_fusion.4
  180.3 1.0 add_select_fusion.4
  187.4 183.6 %all-reduce.2.cloned.1.call-done = f32[1,16,4096]{2,1,0:T(8,128)} async-done(((f32[1,16,4096]{2,1,0:T(8,128)}), f32[1,16,4096]{2,1,0:T(8,128)}) %all-reduce.2.cloned.1.call-update) | async-done | bytes 262160 | tf_op jit(solution)/shard_map/psum | solution.py:25
  371.3 1.3 fusion.2
  372.6 44.5 %all-gather.5.cloned.1.call-done = f32[8,16,4096]{2,1,0:T(8,128)} async-done(((f32[1,16,4096]{2,1,0:T(8,128)}), f32[8,16,4096]{2,1,0:T(8,128)}) %all-gather.5.cloned.1.call-update) | async-done | bytes 2097168 | tf_op jit(solution)/shard_map/all_gather | solution.py:12
  417.2 8.4 %while.29 = (s32[]{:T(128)}, f32[16,4096]{1,0:T(8,128)S(1)}, s32[]{:T(128)}, f32[8,16,4096]{2,1,0:T(8,128)}, s32[]{:T(128)}, /*index=5*/s32[]{:T(128)}) while((s32[]{:T(128)}, f32[16,4096]{1,0:T(8,128)S(1)}, s32[]{:T(128)}, f32[8,16,4096]{2,1,0:T(8,128)}, s32[]{:T(128)}, /*index=5*/s32[]{:T(128)}) %tuple.63), condition=%wide.region_4.5_spmd.clone, body=%wide.region_3.4_spmd.clone.sunk | while | flops 196612 | bytes 786525 | solution.py:20
  420.3 1.0 add_select_fusion.5
  424.6 1.0 add_select_fusion.5
  (38 shorter events, 20.7 us)
Async XLA Ops:
  6.5 112.4 %all-gather.3.cloned.1.call-start = ((), (), s32[]{:S(2)}) async-start(), calls=%async_computation | async-start | bytes 17039360 | tf_op jit(solution)/shard_map/all_gather | solution.py:12
  9.0 362.0 %copy-start = (bf16[256,1024]{1,0:T(8,128)(2,1)S(1)}, bf16[256,1024]{1,0:T(8,128)(2,1)}, u32[]{:S(2)}) copy-start(bf16[256,1024]{1,0:T(8,128)(2,1)} %param.7) | copy-start | bytes 1572868
  10.2 360.8 %all-reduce.2.cloned.1.call-start = ((), (), s32[]{:S(2)}) async-start(), calls=%async_computation.1 | async-start | bytes 524288 | tf_op jit(solution)/shard_map/psum | solution.py:25
  187.4 229.8 %all-gather.5.cloned.1.call-start = ((), (), s32[]{:S(2)}) async-start(), calls=%async_computation.2 | async-start | bytes 2359296 | tf_op jit(solution)/shard_map/all_gather | solution.py:12
Sparse Core Ops, SparseCore 0:
  10.7 108.1 all-gather.2
  187.5 183.5 all-reduce.1
  373.3 43.8 all-gather.4
where the time goes:
time: 436 us; the launch traced here: 434 us
  waiting for transfers between devices  337 us (77%)
  other arithmetic  75.3 us (17%)
  between operations  13.2 us (3%)
  local copies, waits for them, and re-layouts  5.02 us (1%)
    psum x1, waiting for transfers between devices, spread(): return lax.psum(block, axis)  184 us
    all_gather x2, waiting for transfers between devices, carried_in(): everything = lax.all_gather(x, axis)  153 us
    select_n x72, other arithmetic, step(): return jnp.where(reached, new, before)  74.4 us
  transfers between devices with their start and end apart: 3, of which 3 were waited for; matrix products, arithmetic and copies ran while one was open for 0% of the time, Pallas kernels for 0%

commit v1 on v0

v1 whole, which is shorter than its diff:
```python
import functools

import jax
import jax.numpy as jnp
from jax import lax
from jax.experimental import pallas as pl
from jax.experimental.pallas import tpu as pltpu
from jax.sharding import PartitionSpec as P

HEAD_DIM = 64
PAIR = 2 * HEAD_DIM
PAIRS = 8
LINE = 16
CHIPS = 8
ROWS = 32
BF16 = jnp.bfloat16
F32 = jnp.float32
MESH = pl.DeviceIdType.MESH


def dot(a, b, contract):
    return lax.dot_general(a, b, (contract, ((), ())), preferred_element_type=F32)


def attend_kernel(
    nx, nz, q_hbm, k_hbm, v_hbm, o_ref,
    q, k, v, intra, s_out, s_in, t_out, t_in, z_out, z_in, p_out, p_in,
    in_sem, s_send, s_recv, t_send, t_recv, z_send, z_recv, p_send, p_recv,
):
    tokens = q.shape[0]
    half = tokens // 2
    wide = lax.axis_index("wide")
    z = lax.axis_index("chain")
    x = wide // LINE
    a = lax.rem(wide, LINE)
    y = a // 2
    core = lax.rem(a, 2)
    base = x * LINE

    loads = []
    for i, (src, dst) in enumerate(((k_hbm, k), (v_hbm, v), (q_hbm, q))):
        load = pltpu.make_async_copy(src, dst, in_sem.at[i])
        load.start()
        loads.append(load)

    barrier = pltpu.get_barrier_semaphore()
    for i in range(1, LINE):
        pl.semaphore_signal(
            barrier, inc=1, device_id={"wide": base + lax.rem(a + i, LINE)}, device_id_type=MESH
        )
    for i in range(1, nx):
        pl.semaphore_signal(
            barrier, inc=1, device_id={"wide": lax.rem(x + i, nx) * LINE + a}, device_id_type=MESH
        )
    for i in range(1, nz):
        pl.semaphore_signal(
            barrier, inc=1, device_id={"chain": lax.rem(z + i, nz)}, device_id_type=MESH
        )

    low = lax.broadcasted_iota(jnp.int32, (HEAD_DIM, PAIR), 1) < HEAD_DIM

    def pair_state(p):
        cols = pl.ds(pl.multiple_of(p * PAIR, PAIR), PAIR)
        both = dot(k[:, cols], v[:, cols], ((0,), (0,)))
        packed = jnp.where(low, both[:HEAD_DIM], both[HEAD_DIM:])
        return packed.astype(BF16).reshape(2, ROWS, PAIR)

    def send_piece(dest):
        pltpu.make_async_remote_copy(
            src_ref=s_out.at[dest], dst_ref=s_in.at[a], send_sem=s_send, recv_sem=s_recv,
            device_id={"wide": base + dest}, device_id_type=MESH,
        ).start()

    loads[0].wait()
    loads[1].wait()
    first = True
    for s in (4, 3, 5, 2, 6, 1, 7):
        p = lax.rem(y + s, CHIPS)
        s_out[pl.ds(2 * p, 2)] = pair_state(p)
        if first:
            pl.semaphore_wait(barrier, LINE - 1 + nx - 1 + nz - 1)
            first = False
        send_piece(2 * p)
        send_piece(2 * p + 1)
    s_out[pl.ds(2 * y, 2)] = pair_state(y)
    send_piece(2 * y + 1 - core)
    s_in[a] = s_out[a]

    loads[2].wait()

    upper = lax.broadcasted_iota(jnp.int32, (half, half), 0) >= lax.broadcasted_iota(
        jnp.int32, (half, half), 1
    )
    lower = lax.broadcasted_iota(jnp.int32, (half, tokens), 0) + half >= lax.broadcasted_iota(
        jnp.int32, (half, tokens), 1
    )
    lanes = lax.broadcasted_iota(jnp.int32, (1, PAIR), 1)
    keep = [
        jnp.where(lanes < HEAD_DIM, 1.0, 0.0).astype(BF16),
        jnp.where(lanes >= HEAD_DIM, 1.0, 0.0).astype(BF16),
    ]

    def intra_pair(p):
        cols = slice(p * PAIR, (p + 1) * PAIR)
        top = bottom = 0.0
        for h in range(2):
            kh = k[:, cols] * keep[h]
            vh = v[:, cols] * keep[h]
            s_top = dot(q[:half, cols], kh[:half], ((1,), (1,)))
            s_top = jnp.where(upper, s_top, 0.0).astype(BF16)
            s_bot = dot(q[half:, cols], kh, ((1,), (1,)))
            s_bot = jnp.where(lower, s_bot, 0.0).astype(BF16)
            top = top + dot(s_top, vh[:half], ((1,), (0,)))
            bottom = bottom + dot(s_bot, vh, ((1,), (0,)))
        intra[:half, cols] = top
        intra[half:, cols] = bottom

    for p in range(4):
        intra_pair(p)

    pltpu.make_async_copy(s_in.at[: LINE - 1], s_in.at[: LINE - 1], s_recv).wait()
    total = s_in[0].astype(F32)
    for i in range(1, LINE):
        total = total + s_in[i].astype(F32)
    t_out[...] = total
    for i in range(1, nx):
        pltpu.make_async_remote_copy(
            src_ref=t_out, dst_ref=t_in.at[x], send_sem=t_send.at[i], recv_sem=t_recv,
            device_id={"wide": lax.rem(x + i, nx) * LINE + a}, device_id_type=MESH,
        ).start()
    t_in[x] = total

    for p in range(4, 6):
        intra_pair(p)

    pltpu.make_async_copy(t_in.at[: nx - 1], t_in.at[: nx - 1], t_recv).wait()
    plane = jnp.zeros((ROWS, PAIR), F32)
    before = jnp.zeros((ROWS, PAIR), F32)
    for i in range(nx):
        plane = plane + t_in[i]
        before = before + jnp.where(i < x, t_in[i], 0.0)
    z_out[...] = plane

    def z_copy(other):
        return pltpu.make_async_remote_copy(
            src_ref=z_out, dst_ref=z_in.at[z], send_sem=z_send.at[other], recv_sem=z_recv.at[z],
            device_id={"chain": other}, device_id_type=MESH,
        )

    def z_start(i, _):
        z_copy(z + i).start()
        return 0

    lax.fori_loop(1, nz - z, z_start, 0)

    for p in range(6, 8):
        intra_pair(p)

    def z_take(i, acc):
        pltpu.make_async_copy(z_in.at[i], z_in.at[i], z_recv.at[i]).wait()
        return acc + z_in[i]

    run = lax.fori_loop(0, z, z_take, before)
    for i in range(LINE):
        p_out[i] = run.astype(BF16)
        if i + 1 < LINE:
            run = run + s_in[i].astype(F32)
    p_in[a] = p_out[a]
    for i in (8, 9, 7, 10, 6, 11, 5, 12, 4, 13, 3, 14, 2, 15, 1):
        dest = lax.rem(a + i, LINE)
        pltpu.make_async_remote_copy(
            src_ref=p_out.at[dest], dst_ref=p_in.at[a], send_sem=p_send, recv_sem=p_recv,
            device_id={"wide": base + dest}, device_id_type=MESH,
        ).start()

    mean = jnp.where(
        (lax.broadcasted_iota(jnp.int32, (PAIR, PAIR), 0) < HEAD_DIM)
        == (lax.broadcasted_iota(jnp.int32, (PAIR, PAIR), 1) < HEAD_DIM),
        1.0 / HEAD_DIM, 0.0,
    ).astype(BF16)
    pltpu.make_async_copy(p_in.at[: LINE - 1], p_in.at[: LINE - 1], p_recv).wait()
    for p in range(PAIRS):
        cols = slice(p * PAIR, (p + 1) * PAIR)
        prefix = p_in[2 * p : 2 * p + 2].reshape(HEAD_DIM, PAIR)
        prefix = jnp.concatenate([prefix * keep[0], prefix * keep[1]], axis=0)
        value = intra[:, cols] + dot(q[:, cols], prefix, ((1,), (0,)))
        square = value * value
        coarse = square.astype(BF16)
        fine = (square - coarse.astype(F32)).astype(BF16)
        var = dot(coarse, mean, ((1,), (0,))) + dot(fine, mean, ((1,), (0,)))
        o_ref[:, cols] = (value * lax.rsqrt(var + 1e-06)).astype(BF16)

    pltpu.make_async_copy(s_out.at[: LINE - 1], s_out.at[: LINE - 1], s_send).wait()
    for i in range(1, nx):
        pltpu.make_async_copy(t_out, t_out, t_send.at[i]).wait()

    def z_done(i, _):
        pltpu.make_async_copy(z_out, z_out, z_send.at[z + i]).wait()
        return 0

    lax.fori_loop(1, nz - z, z_done, 0)
    pltpu.make_async_copy(p_out.at[: LINE - 1], p_out.at[: LINE - 1], p_send).wait()


def solution(mesh):
    nx = mesh.shape["wide"] // LINE
    nz = mesh.shape["chain"]

    def per_device(queries, keys, values):
        tokens, width = queries.shape
        dma = pltpu.SemaphoreType.DMA
        return pl.pallas_call(
            functools.partial(attend_kernel, nx, nz),
            out_shape=jax.ShapeDtypeStruct((tokens, width), BF16),
            in_specs=[pl.BlockSpec(memory_space=pltpu.HBM)] * 3,
            out_specs=pl.BlockSpec(memory_space=pltpu.VMEM),
            scratch_shapes=[
                pltpu.VMEM((tokens, width), BF16),
                pltpu.VMEM((tokens, width), BF16),
                pltpu.VMEM((tokens, width), BF16),
                pltpu.VMEM((tokens, width), F32),
                pltpu.VMEM((LINE, ROWS, PAIR), BF16),
                pltpu.VMEM((LINE, ROWS, PAIR), BF16),
                pltpu.VMEM((ROWS, PAIR), F32),
                pltpu.VMEM((nx, ROWS, PAIR), F32),
                pltpu.VMEM((ROWS, PAIR), F32),
                pltpu.VMEM((nz, ROWS, PAIR), F32),
                pltpu.VMEM((LINE, ROWS, PAIR), BF16),
                pltpu.VMEM((LINE, ROWS, PAIR), BF16),
                dma((3,)),
                dma,
                dma,
                dma((nx,)),
                dma,
                dma((nz,)),
                dma((nz,)),
                dma,
                dma,
            ],
            compiler_params=pltpu.CompilerParams(
                collective_id=0, has_side_effects=True, vmem_limit_bytes=32 << 20
            ),
        )(*(pltpu.with_memory_space_constraint(t, pltpu.HBM) for t in (queries, keys, values)))

    placed = P(("chain", "wide"), None)
    return jax.shard_map(
        per_device, mesh=mesh, in_specs=(placed,) * 3, out_specs=placed, check_vma=False
    )
```

time: 436 us -> 31.6 us (0.07)
  the two profiles are of different devices: /device:TPU:2 before, /device:TPU:1 now
where the time goes in v1:
time: 31.6 us; the launch traced here: 31.4 us
  Pallas kernels  30.6 us (97%)
  local copies, waits for them, and re-layouts  0.8 us (3%)
    pallas_call x1, Pallas kernels, per_device(): pl.pallas_call(functools.partial(attend_kernel, nx, nz), out_shape=jax.Sh...  30.6 us
    unnamed x1, local copies, waits for them, and re-layouts  0.8 us

profile of v1, /device:TPU:1, one launch (start us, length us, event | category | flops | bytes accessed | tf_op | source)
XLA Modules:
  0.0 31.4 jit_solution(9291635667086668562)
XLA Ops:
  0.0 30.6 %shard_map.37 = bf16[256,1024]{1,0:T(8,128)(2,1)S(1)} custom-call(bf16[256,1024]{1,0:T(8,128)(2,1)} %q_hbm.1, bf16[256,1024]{1,0:T(8,128)(2,1)} %k_hbm.1, bf16[256,1024]{1,0:T(8,128)(2,1)} %v_hbm.1), custom_call_target="tpu_custom_call" | custom-call | tf_op jit(solution)/shard_map/pallas_call | solution.py:212
  30.6 0.8 %copy.5 = bf16[256,1024]{1,0:T(8,128)(2,1)} copy(bf16[256,1024]{1,0:T(8,128)(2,1)S(1)} %shard_map.37) | data formatting | bytes 1048576

commit v2 on v0

v2 whole, which is shorter than its diff:
```python
import functools

import jax
import jax.numpy as jnp
from jax import lax
from jax.experimental import pallas as pl
from jax.experimental.pallas import tpu as pltpu
from jax.sharding import PartitionSpec as P

HEAD_DIM = 64
PAIR = 2 * HEAD_DIM
PAIRS = 8
HALF = PAIRS // 2
CHIPS = 8
ROWS = 8
STATE = HALF * HEAD_DIM
QUAD = 2 * PAIR
BF16 = jnp.bfloat16
F32 = jnp.float32
MESH = pl.DeviceIdType.MESH


def dot(a, b, contract):
    return lax.dot_general(a, b, (contract, ((), ())), preferred_element_type=F32)


def attend_kernel(
    nx, nz, q_hbm, k_hbm, v_hbm, o_ref,
    q, k, v, intra, given, mine, theirs, first, s_out, s_in, z_out, z_in, p_out, p_in, p_other,
    in_sem, mate_send, mate_recv, s_send, s_recv, z_send, z_recv, p_send, p_recv, f_send, f_recv,
    mate_here, all_here, z_ready,
):
    tokens = q.shape[0]
    row_half = tokens // 2
    members = nx * CHIPS
    wide = lax.axis_index("wide")
    z = lax.axis_index("chain")
    chip = wide // 2
    core = lax.rem(wide, 2)
    mate = {"wide": 2 * chip + 1 - core}
    mid = nz // 2
    z_from = jnp.where(z < mid, 0, mid - 1)
    z_to = jnp.where(z < mid - 1, mid, nz)
    x, y = chip // CHIPS, lax.rem(chip, CHIPS)
    away = [(i, j) for i in range(nx) for j in range(CHIPS) if i or j]
    away.sort(key=lambda d: -min(d[0], nx - d[0]) - min(d[1], CHIPS - d[1]))
    peers = [lax.rem(x + i, nx) * CHIPS + lax.rem(y + j, CHIPS) for i, j in away]

    def plane_id(chip):
        return {"wide": 2 * chip + core}

    def z_id(i):
        return {"chain": i}

    loads = []
    for c in range(4):
        half = 1 - core if c < 2 else core
        cols = pl.ds(pl.multiple_of(half * (HALF * PAIR) + (c % 2) * QUAD, QUAD), QUAD)
        pair = [
            pltpu.make_async_copy(k_hbm.at[:, cols], k.at[:, cols], in_sem.at[2 * c]),
            pltpu.make_async_copy(v_hbm.at[:, cols], v.at[:, cols], in_sem.at[2 * c + 1]),
        ]
        for load in pair:
            load.start()
        loads.append(pair)
    q_load = pltpu.make_async_copy(q_hbm, q, in_sem.at[8])
    q_load.start()

    barrier = pltpu.get_barrier_semaphore()

    @pl.when(core == 1)
    def _():
        pl.semaphore_signal(barrier, inc=1, device_id=mate, device_id_type=MESH)

    @pl.when(core == 0)
    def _():
        pl.semaphore_wait(barrier, 1)
        pl.semaphore_signal(mate_here, inc=1, device_id=mate, device_id_type=MESH)

    @pl.when(core == 1)
    def _():
        pl.semaphore_wait(mate_here, 1)
        for chip_there in peers:
            pl.semaphore_signal(
                barrier, inc=1, device_id=plane_id(chip_there), device_id_type=MESH
            )

        def greet(i, _):
            pl.semaphore_signal(barrier, inc=1, device_id=z_id(i), device_id_type=MESH)
            return 0

        lax.fori_loop(z + 1, z_to, greet, 0)

    low = lax.broadcasted_iota(jnp.int32, (HEAD_DIM, PAIR), 1) < HEAD_DIM

    def pair_state(half, j):
        cols = pl.ds(pl.multiple_of((half * HALF + j) * PAIR, PAIR), PAIR)
        both = dot(k[:, cols], v[:, cols], ((0,), (0,)))
        return jnp.where(low, both[:HEAD_DIM], both[HEAD_DIM:])

    def half_state(half, first_load, out):
        for j in range(HALF):
            if j % 2 == 0:
                for load in loads[first_load + j // 2]:
                    load.wait()
            out[j * HEAD_DIM : (j + 1) * HEAD_DIM] = pair_state(half, j)

    half_state(1 - core, 0, given)

    swap = pltpu.make_async_remote_copy(
        src_ref=given, dst_ref=theirs, send_sem=mate_send.at[0],
        recv_sem=mate_recv.at[0], device_id=mate, device_id_type=MESH,
    )
    swap.start()
    half_state(core, 2, mine)
    extra = pltpu.make_async_remote_copy(
        src_ref=mine, dst_ref=first, send_sem=mate_send.at[1], recv_sem=mate_recv.at[1],
        device_id=mate, device_id_type=MESH,
    )

    @pl.when(core == 0)
    def _():
        extra.start()

    swap.wait_recv()
    for i in range(members):
        rows = slice(i * ROWS, (i + 1) * ROWS)
        s_out[i] = (mine[rows] + theirs[rows]).astype(BF16)

    @pl.when(core == 1)
    def _():
        pl.semaphore_wait(barrier, members - 1 + z - z_from)
        pl.semaphore_signal(all_here, inc=1, device_id=mate, device_id_type=MESH)

    @pl.when(core == 0)
    def _():
        pl.semaphore_wait(all_here, 1)

    for chip_there in peers:
        pltpu.make_async_remote_copy(
            src_ref=s_out.at[chip_there], dst_ref=s_in.at[chip], send_sem=s_send, recv_sem=s_recv,
            device_id=plane_id(chip_there), device_id_type=MESH,
        ).start()

    s_in[chip] = s_out[chip]

    def answer_z(i, _):
        pl.semaphore_signal(z_ready.at[z], inc=1, device_id=z_id(i), device_id_type=MESH)
        return 0

    lax.fori_loop(z_from, z, answer_z, 0)

    upper = lax.broadcasted_iota(jnp.int32, (row_half, row_half), 0) >= lax.broadcasted_iota(
        jnp.int32, (row_half, row_half), 1
    )
    lower = lax.broadcasted_iota(
        jnp.int32, (row_half, tokens), 0
    ) + row_half >= lax.broadcasted_iota(jnp.int32, (row_half, tokens), 1)
    lanes = lax.broadcasted_iota(jnp.int32, (1, PAIR), 1)
    keep = [
        jnp.where(lanes < HEAD_DIM, 1.0, 0.0).astype(BF16),
        jnp.where(lanes >= HEAD_DIM, 1.0, 0.0).astype(BF16),
    ]

    def spread(packed):
        return jnp.concatenate([packed * keep[0], packed * keep[1]], axis=0)

    def intra_pair(p, _):
        cols = pl.ds(pl.multiple_of(p * PAIR, PAIR), PAIR)
        qp, kp, vp = q[:, cols], k[:, cols], v[:, cols]
        top = bottom = 0.0
        for h in range(2):
            kh = kp * keep[h]
            vh = vp * keep[h]
            s_top = dot(qp[:row_half], kh[:row_half], ((1,), (1,)))
            s_top = jnp.where(upper, s_top, 0.0).astype(BF16)
            s_bot = dot(qp[row_half:], kh, ((1,), (1,)))
            s_bot = jnp.where(lower, s_bot, 0.0).astype(BF16)
            top = top + dot(s_top, vh[:row_half], ((1,), (0,)))
            bottom = bottom + dot(s_bot, vh, ((1,), (0,)))
        intra[:row_half, cols] = top
        intra[row_half:, cols] = bottom
        return 0

    q_load.wait()
    lax.fori_loop(0, PAIRS, intra_pair, 0)

    @pl.when(core == 1)
    def _():
        extra.wait_recv()
        for p in range(PAIRS):
            cols = slice(p * PAIR, (p + 1) * PAIR)
            rows = slice((p % HALF) * HEAD_DIM, (p % HALF + 1) * HEAD_DIM)
            state = (first if p < HALF else theirs)[rows].astype(BF16)
            intra[:, cols] += dot(q[:, cols], spread(state), ((1,), (0,)))

    @pl.when(core == 0)
    def _():
        extra.wait_send()

    pltpu.make_async_copy(s_in.at[: members - 1], s_in.at[: members - 1], s_recv).wait()
    plane = s_in[0].astype(F32)
    for i in range(1, members):
        plane = plane + s_in[i].astype(F32)

    def z_start(i, _):
        pl.semaphore_wait(z_ready.at[i], 1)
        pltpu.make_async_remote_copy(
            src_ref=z_out, dst_ref=z_in.at[z], send_sem=z_send.at[i], recv_sem=z_recv.at[z],
            device_id=z_id(i), device_id_type=MESH,
        ).start()
        return 0

    def z_take(i, acc):
        pltpu.make_async_copy(z_in.at[i], z_in.at[i], z_recv.at[i]).wait()
        return acc + z_in[i]

    @pl.when(z != mid - 1)
    def _():
        z_out[...] = plane
        lax.fori_loop(z + 1, z_to, z_start, 0)

    run = lax.fori_loop(z_from, z, z_take, jnp.zeros((ROWS, PAIR), F32))

    @pl.when(z == mid - 1)
    def _():
        z_out[...] = run + plane
        lax.fori_loop(z + 1, z_to, z_start, 0)

    for i in range(members):
        p_out[i] = run.astype(BF16)
        if i + 1 < members:
            run = run + s_in[i].astype(F32)

    for chip_there in peers:
        pltpu.make_async_remote_copy(
            src_ref=p_out.at[chip_there], dst_ref=p_in.at[chip], send_sem=p_send, recv_sem=p_recv,
            device_id=plane_id(chip_there), device_id_type=MESH,
        ).start()

    p_in[chip] = p_out[chip]

    swap.wait_send()
    pltpu.make_async_copy(s_out.at[: members - 1], s_out.at[: members - 1], s_send).wait()

    def z_done(i, _):
        pltpu.make_async_copy(z_out, z_out, z_send.at[i]).wait()
        return 0

    lax.fori_loop(z + 1, z_to, z_done, 0)

    mean = jnp.where(
        lax.broadcasted_iota(jnp.int32, (QUAD, QUAD), 0) // HEAD_DIM
        == lax.broadcasted_iota(jnp.int32, (QUAD, QUAD), 1) // HEAD_DIM,
        1.0 / HEAD_DIM, 0.0,
    ).astype(BF16)
    zeros = jnp.zeros((PAIR, PAIR), BF16)

    def finish(half, pieces):
        for j in range(0, HALF, 2):
            cols = pl.ds(pl.multiple_of((half * HALF + j) * PAIR, QUAD), QUAD)
            n = HEAD_DIM // ROWS
            one = spread(pieces[j * n : (j + 1) * n].reshape(HEAD_DIM, PAIR))
            two = spread(pieces[(j + 1) * n : (j + 2) * n].reshape(HEAD_DIM, PAIR))
            prefix = jnp.concatenate(
                [jnp.concatenate([one, zeros], axis=1), jnp.concatenate([zeros, two], axis=1)],
                axis=0,
            )
            value = intra[:, cols] + dot(q[:, cols], prefix, ((1,), (0,)))
            square = value * value
            coarse = square.astype(BF16)
            fine = (square - coarse.astype(F32)).astype(BF16)
            var = dot(coarse, mean, ((1,), (0,))) + dot(fine, mean, ((1,), (0,)))
            o_ref[:, cols] = (value * lax.rsqrt(var + 1e-06)).astype(BF16)

    pltpu.make_async_copy(p_in.at[: members - 1], p_in.at[: members - 1], p_recv).wait()
    forward = pltpu.make_async_remote_copy(
        src_ref=p_in, dst_ref=p_other, send_sem=f_send, recv_sem=f_recv,
        device_id=mate, device_id_type=MESH,
    )
    forward.start()
    finish(core, p_in)
    forward.wait_recv()
    finish(1 - core, p_other)
    forward.wait_send()
    pltpu.make_async_copy(p_out.at[: members - 1], p_out.at[: members - 1], p_send).wait()


def solution(mesh):
    nx = mesh.shape["wide"] // (2 * CHIPS)
    nz = mesh.shape["chain"]
    members = nx * CHIPS

    def per_device(queries, keys, values):
        tokens, width = queries.shape
        dma = pltpu.SemaphoreType.DMA
        plain = pltpu.SemaphoreType.REGULAR
        in_hbm = [pltpu.with_memory_space_constraint(t, pltpu.HBM) for t in (queries, keys, values)]
        return pl.pallas_call(
            functools.partial(attend_kernel, nx, nz),
            out_shape=jax.ShapeDtypeStruct((tokens, width), BF16),
            in_specs=[pl.BlockSpec(memory_space=pltpu.HBM)] * 3,
            out_specs=pl.BlockSpec(memory_space=pltpu.VMEM),
            scratch_shapes=[
                pltpu.VMEM((tokens, width), BF16),
                pltpu.VMEM((tokens, width), BF16),
                pltpu.VMEM((tokens, width), BF16),
                pltpu.VMEM((tokens, width), F32),
                pltpu.VMEM((STATE, PAIR), F32),
                pltpu.VMEM((STATE, PAIR), F32),
                pltpu.VMEM((STATE, PAIR), F32),
                pltpu.VMEM((STATE, PAIR), F32),
                pltpu.VMEM((members, ROWS, PAIR), BF16),
                pltpu.VMEM((members, ROWS, PAIR), BF16),
                pltpu.VMEM((ROWS, PAIR), F32),
                pltpu.VMEM((nz, ROWS, PAIR), F32),
                pltpu.VMEM((members, ROWS, PAIR), BF16),
                pltpu.VMEM((members, ROWS, PAIR), BF16),
                pltpu.VMEM((members, ROWS, PAIR), BF16),
                dma((9,)),
                dma((2,)),
                dma((2,)),
                dma,
                dma,
                dma((nz,)),
                dma((nz,)),
                dma,
                dma,
                dma,
                dma,
                plain,
                plain,
                plain((nz,)),
            ],
            compiler_params=pltpu.CompilerParams(
                collective_id=0, has_side_effects=True, vmem_limit_bytes=32 << 20
            ),
        )(*in_hbm)

    placed = P(("chain", "wide"), None)
    return jax.shard_map(
        per_device, mesh=mesh, in_specs=(placed,) * 3, out_specs=placed, check_vma=False
    )
```

time: 436 us -> 26.6 us (0.06)
  the two profiles are of different devices: /device:TPU:2 before, /device:TPU:385 now
where the time goes in v2:
time: 26.6 us; the launch traced here: 26.5 us
  Pallas kernels  25.7 us (97%)
  local copies, waits for them, and re-layouts  0.8 us (3%)
    pallas_call x1, Pallas kernels, per_device(): pl.pallas_call(functools.partial(attend_kernel, nx, nz), out_shape=jax.Sh...  25.7 us
    unnamed x1, local copies, waits for them, and re-layouts  0.8 us

profile of v2, /device:TPU:385, one launch (start us, length us, event | category | flops | bytes accessed | tf_op | source)
XLA Modules:
  0.0 26.5 jit_solution(3028611744340220795)
XLA Ops:
  0.0 25.7 %shard_map.37 = bf16[256,1024]{1,0:T(8,128)(2,1)S(1)} custom-call(bf16[256,1024]{1,0:T(8,128)(2,1)} %q_hbm.1, bf16[256,1024]{1,0:T(8,128)(2,1)} %k_hbm.1, bf16[256,1024]{1,0:T(8,128)(2,1)} %v_hbm.1), custom_call_target="tpu_custom_call" | custom-call | tf_op jit(solution)/shard_map/pallas_call | solution.py:299
  25.7 0.8 %copy.5 = bf16[256,1024]{1,0:T(8,128)(2,1)} copy(bf16[256,1024]{1,0:T(8,128)(2,1)S(1)} %shard_map.37) | data formatting | bytes 1048576

commit v3 on v2

--- a/solution.py
+++ b/solution.py
@@ -12,7 +12,9 @@
 PAIRS = 8
 HALF = PAIRS // 2
 CHIPS = 8
-ROWS = 8
+OWNED = (0, 1)
+GREETED = (5, 4, 6, 3, 7, 2, 1, 0)
+ROWS = 64 // len(OWNED)
 STATE = HALF * HEAD_DIM
 QUAD = 2 * PAIR
 BF16 = jnp.bfloat16
@@ -33,24 +35,38 @@
     tokens = q.shape[0]
     row_half = tokens // 2
     members = nx * CHIPS
+    owners = nx * len(OWNED)
     wide = lax.axis_index("wide")
     z = lax.axis_index("chain")
     chip = wide // 2
     core = lax.rem(wide, 2)
     mate = {"wide": 2 * chip + 1 - core}
-    mid = nz // 2
-    z_from = jnp.where(z < mid, 0, mid - 1)
-    z_to = jnp.where(z < mid - 1, mid, nz)
     x, y = chip // CHIPS, lax.rem(chip, CHIPS)
-    away = [(i, j) for i in range(nx) for j in range(CHIPS) if i or j]
-    away.sort(key=lambda d: -min(d[0], nx - d[0]) - min(d[1], CHIPS - d[1]))
-    peers = [lax.rem(x + i, nx) * CHIPS + lax.rem(y + j, CHIPS) for i, j in away]
+    place = sum(jnp.where(y == there, i, 0) for i, there in enumerate(OWNED))
+    owns = functools.reduce(jnp.logical_or, [y == there for there in OWNED])
+    owner = x * len(OWNED) + place
+    near = sorted(range(nx), key=lambda d: min(d, nx - d))
+    far = near[::-1]
 
     def plane_id(chip):
         return {"wide": 2 * chip + core}
 
     def z_id(i):
         return {"chain": i}
+
+    def to_plane(columns, across, act):
+        for there in columns:
+            for d in across:
+                chip_there = lax.rem(x + d, nx) * CHIPS + there
+                if d:
+                    act(chip_there)
+                else:
+                    pl.when(there != y)(functools.partial(act, chip_there))
+
+    def owner_of(chip):
+        column = lax.rem(chip, CHIPS)
+        place = sum(jnp.where(column == there, i, 0) for i, there in enumerate(OWNED))
+        return chip // CHIPS * len(OWNED) + place
 
     loads = []
     for c in range(4):
@@ -72,6 +88,22 @@
     def _():
         pl.semaphore_signal(barrier, inc=1, device_id=mate, device_id_type=MESH)
 
+    def greet(chip_there, plane_there=z):
+        pl.semaphore_signal(
+            barrier, inc=1, device_id={"wide": 2 * chip_there + 1, "chain": plane_there},
+            device_id_type=MESH,
+        )
+
+    @pl.when(owns)
+    def _():
+        to_plane(GREETED, far, greet)
+
+        def greet_later(i, _):
+            greet(chip, i)
+            return 0
+
+        lax.fori_loop(z + 1, nz, greet_later, 0)
+
     @pl.when(core == 0)
     def _():
         pl.semaphore_wait(barrier, 1)
@@ -80,16 +112,6 @@
     @pl.when(core == 1)
     def _():
         pl.semaphore_wait(mate_here, 1)
-        for chip_there in peers:
-            pl.semaphore_signal(
-                barrier, inc=1, device_id=plane_id(chip_there), device_id_type=MESH
-            )
-
-        def greet(i, _):
-            pl.semaphore_signal(barrier, inc=1, device_id=z_id(i), device_id_type=MESH)
-            return 0
-
-        lax.fori_loop(z + 1, z_to, greet, 0)
 
     low = lax.broadcasted_iota(jnp.int32, (HEAD_DIM, PAIR), 1) < HEAD_DIM
 
@@ -123,32 +145,43 @@
         extra.start()
 
     swap.wait_recv()
-    for i in range(members):
+    for i in range(owners):
         rows = slice(i * ROWS, (i + 1) * ROWS)
         s_out[i] = (mine[rows] + theirs[rows]).astype(BF16)
 
+    @pl.when((core == 1) & owns)
+    def _():
+        pl.semaphore_wait(barrier, 2 * (owners - 1 + z))
+
+    @pl.when((core == 1) & jnp.logical_not(owns))
+    def _():
+        pl.semaphore_wait(barrier, 2 * owners)
+
     @pl.when(core == 1)
     def _():
-        pl.semaphore_wait(barrier, members - 1 + z - z_from)
         pl.semaphore_signal(all_here, inc=1, device_id=mate, device_id_type=MESH)
 
     @pl.when(core == 0)
     def _():
         pl.semaphore_wait(all_here, 1)
 
-    for chip_there in peers:
+    def send_piece(there):
         pltpu.make_async_remote_copy(
-            src_ref=s_out.at[chip_there], dst_ref=s_in.at[chip], send_sem=s_send, recv_sem=s_recv,
-            device_id=plane_id(chip_there), device_id_type=MESH,
+            src_ref=s_out.at[owner_of(there)], dst_ref=s_in.at[chip], send_sem=s_send, recv_sem=s_recv,
+            device_id=plane_id(there), device_id_type=MESH,
         ).start()
 
-    s_in[chip] = s_out[chip]
-
-    def answer_z(i, _):
-        pl.semaphore_signal(z_ready.at[z], inc=1, device_id=z_id(i), device_id_type=MESH)
-        return 0
-
-    lax.fori_loop(z_from, z, answer_z, 0)
+    to_plane(OWNED, far, send_piece)
+
+    @pl.when(owns)
+    def _():
+        s_in[chip] = s_out[owner]
+
+        def answer_z(i, _):
+            pl.semaphore_signal(z_ready.at[z], inc=1, device_id=z_id(i), device_id_type=MESH)
+            return 0
+
+        lax.fori_loop(0, z, answer_z, 0)
 
     upper = lax.broadcasted_iota(jnp.int32, (row_half, row_half), 0) >= lax.broadcasted_iota(
         jnp.int32, (row_half, row_half), 1
@@ -198,11 +231,6 @@
     def _():
         extra.wait_send()
 
-    pltpu.make_async_copy(s_in.at[: members - 1], s_in.at[: members - 1], s_recv).wait()
-    plane = s_in[0].astype(F32)
-    for i in range(1, members):
-        plane = plane + s_in[i].astype(F32)
-
     def z_start(i, _):
         pl.semaphore_wait(z_ready.at[i], 1)
         pltpu.make_async_remote_copy(
@@ -215,40 +243,42 @@
         pltpu.make_async_copy(z_in.at[i], z_in.at[i], z_recv.at[i]).wait()
         return acc + z_in[i]
 
-    @pl.when(z != mid - 1)
-    def _():
-        z_out[...] = plane
-        lax.fori_loop(z + 1, z_to, z_start, 0)
-
-    run = lax.fori_loop(z_from, z, z_take, jnp.zeros((ROWS, PAIR), F32))
-
-    @pl.when(z == mid - 1)
-    def _():
-        z_out[...] = run + plane
-        lax.fori_loop(z + 1, z_to, z_start, 0)
-
-    for i in range(members):
-        p_out[i] = run.astype(BF16)
-        if i + 1 < members:
-            run = run + s_in[i].astype(F32)
-
-    for chip_there in peers:
-        pltpu.make_async_remote_copy(
-            src_ref=p_out.at[chip_there], dst_ref=p_in.at[chip], send_sem=p_send, recv_sem=p_recv,
-            device_id=plane_id(chip_there), device_id_type=MESH,
-        ).start()
-
-    p_in[chip] = p_out[chip]
-
-    swap.wait_send()
-    pltpu.make_async_copy(s_out.at[: members - 1], s_out.at[: members - 1], s_send).wait()
-
     def z_done(i, _):
         pltpu.make_async_copy(z_out, z_out, z_send.at[i]).wait()
         return 0
 
-    lax.fori_loop(z + 1, z_to, z_done, 0)
-
+    def send_back(there):
+        pltpu.make_async_remote_copy(
+            src_ref=p_out.at[there], dst_ref=p_in.at[owner], send_sem=p_send, recv_sem=p_recv.at[x // 2],
+            device_id=plane_id(there), device_id_type=MESH,
+        ).start()
+
+    def wait_for(buffer, count, sem):
+        pltpu.make_async_copy(buffer.at[:count], buffer.at[:count], sem).wait()
+
+    @pl.when(owns)
+    def _():
+        wait_for(s_in, members - 1, s_recv)
+        plane = s_in[0].astype(F32)
+        for i in range(1, members):
+            plane = plane + s_in[i].astype(F32)
+        z_out[...] = plane
+        lax.fori_loop(z + 1, nz, z_start, 0)
+        run = lax.fori_loop(0, z, z_take, jnp.zeros((ROWS, PAIR), F32))
+        for i in range(members):
+            p_out[i] = run.astype(BF16)
+            if i + 1 < members:
+                run = run + s_in[i].astype(F32)
+        to_plane(range(CHIPS), far, send_back)
+        p_in[owner] = p_out[chip]
+        wait_for(s_out, owners - 1, s_send)
+        lax.fori_loop(z + 1, nz, z_done, 0)
+
+    @pl.when(jnp.logical_not(owns))
+    def _():
+        wait_for(s_out, owners, s_send)
+
+    swap.wait_send()
     mean = jnp.where(
         lax.broadcasted_iota(jnp.int32, (QUAD, QUAD), 0) // HEAD_DIM
         == lax.broadcasted_iota(jnp.int32, (QUAD, QUAD), 1) // HEAD_DIM,
@@ -256,40 +286,57 @@
     ).astype(BF16)
     zeros = jnp.zeros((PAIR, PAIR), BF16)
 
-    def finish(half, pieces):
-        for j in range(0, HALF, 2):
-            cols = pl.ds(pl.multiple_of((half * HALF + j) * PAIR, QUAD), QUAD)
-            n = HEAD_DIM // ROWS
-            one = spread(pieces[j * n : (j + 1) * n].reshape(HEAD_DIM, PAIR))
-            two = spread(pieces[(j + 1) * n : (j + 2) * n].reshape(HEAD_DIM, PAIR))
-            prefix = jnp.concatenate(
-                [jnp.concatenate([one, zeros], axis=1), jnp.concatenate([zeros, two], axis=1)],
-                axis=0,
-            )
-            value = intra[:, cols] + dot(q[:, cols], prefix, ((1,), (0,)))
-            square = value * value
-            coarse = square.astype(BF16)
-            fine = (square - coarse.astype(F32)).astype(BF16)
-            var = dot(coarse, mean, ((1,), (0,))) + dot(fine, mean, ((1,), (0,)))
-            o_ref[:, cols] = (value * lax.rsqrt(var + 1e-06)).astype(BF16)
-
-    pltpu.make_async_copy(p_in.at[: members - 1], p_in.at[: members - 1], p_recv).wait()
-    forward = pltpu.make_async_remote_copy(
-        src_ref=p_in, dst_ref=p_other, send_sem=f_send, recv_sem=f_recv,
-        device_id=mate, device_id_type=MESH,
-    )
-    forward.start()
-    finish(core, p_in)
-    forward.wait_recv()
-    finish(1 - core, p_other)
-    forward.wait_send()
-    pltpu.make_async_copy(p_out.at[: members - 1], p_out.at[: members - 1], p_send).wait()
+    def finish(half, part, pieces):
+        cols = pl.ds(pl.multiple_of((half * HALF + part * 2) * PAIR, QUAD), QUAD)
+        both = pieces[pl.ds(part * share, share)].reshape(2 * HEAD_DIM, PAIR)
+        one, two = spread(both[:HEAD_DIM]), spread(both[HEAD_DIM:])
+        prefix = jnp.concatenate(
+            [jnp.concatenate([one, zeros], axis=1), jnp.concatenate([zeros, two], axis=1)], axis=0
+        )
+        value = intra[:, cols] + dot(q[:, cols], prefix, ((1,), (0,)))
+        square = value * value
+        coarse = square.astype(BF16)
+        fine = (square - coarse.astype(F32)).astype(BF16)
+        var = dot(coarse, mean, ((1,), (0,))) + dot(fine, mean, ((1,), (0,)))
+        o_ref[:, cols] = (value * lax.rsqrt(var + 1e-06)).astype(BF16)
+
+    parts = [x // 2, 1 - x // 2]
+    share = owners // 2
+
+    def forward(part):
+        place = pl.ds(part * share, share)
+        return pltpu.make_async_remote_copy(
+            src_ref=p_in.at[place], dst_ref=p_other.at[place], send_sem=f_send.at[part],
+            recv_sem=f_recv.at[part], device_id=mate, device_id_type=MESH,
+        )
+
+    for step, part in enumerate(parts):
+
+        def arrive(count):
+            wait_for(p_in, count, p_recv.at[part])
+
+        if step == 0:
+            pl.when(owns)(functools.partial(arrive, share - 1))
+            pl.when(jnp.logical_not(owns))(functools.partial(arrive, share))
+        else:
+            arrive(share)
+        forward(part).start()
+        finish(core, part, p_in)
+    for part in parts:
+        forward(part).wait_recv()
+        finish(1 - core, part, p_other)
+    for part in parts:
+        forward(part).wait_send()
+
+    @pl.when(owns)
+    def _():
+        wait_for(p_out, members - 1, p_send)
 
 
 def solution(mesh):
     nx = mesh.shape["wide"] // (2 * CHIPS)
     nz = mesh.shape["chain"]
-    members = nx * CHIPS
+    members, owners = nx * CHIPS, nx * len(OWNED)
 
     def per_device(queries, keys, values):
         tokens, width = queries.shape
@@ -310,13 +357,13 @@
                 pltpu.VMEM((STATE, PAIR), F32),
                 pltpu.VMEM((STATE, PAIR), F32),
                 pltpu.VMEM((STATE, PAIR), F32),
-                pltpu.VMEM((members, ROWS, PAIR), BF16),
+                pltpu.VMEM((owners, ROWS, PAIR), BF16),
                 pltpu.VMEM((members, ROWS, PAIR), BF16),
                 pltpu.VMEM((ROWS, PAIR), F32),
                 pltpu.VMEM((nz, ROWS, PAIR), F32),
                 pltpu.VMEM((members, ROWS, PAIR), BF16),
-                pltpu.VMEM((members, ROWS, PAIR), BF16),
-                pltpu.VMEM((members, ROWS, PAIR), BF16),
+                pltpu.VMEM((owners, ROWS, PAIR), BF16),
+                pltpu.VMEM((owners, ROWS, PAIR), BF16),
                 dma((9,)),
                 dma((2,)),
                 dma((2,)),
@@ -325,9 +372,9 @@
                 dma((nz,)),
                 dma((nz,)),
                 dma,
-                dma,
-                dma,
-                dma,
+                dma((2,)),
+                dma((2,)),
+                dma((2,)),
                 plain,
                 plain,
                 plain((nz,)),

time: 26.6 us -> 25.6 us (0.962)
  the two profiles are of different devices: /device:TPU:385 before, /device:TPU:121 now
where the time goes in v3:
time: 25.6 us; the launch traced here: 25.4 us
  Pallas kernels  24.6 us (96%)
  local copies, waits for them, and re-layouts  0.8 us (3%)
    pallas_call x1, Pallas kernels, per_device(): pl.pallas_call(functools.partial(attend_kernel, nx, nz), out_shape=jax.Sh...  24.6 us
    unnamed x1, local copies, waits for them, and re-layouts  0.8 us

profile of v3, /device:TPU:121, one launch (start us, length us, event | category | flops | bytes accessed | tf_op | source)
XLA Modules:
  0.0 25.4 jit_solution(9145427780125318381)
XLA Ops:
  0.0 24.6 %shard_map.37 = bf16[256,1024]{1,0:T(8,128)(2,1)S(1)} custom-call(bf16[256,1024]{1,0:T(8,128)(2,1)} %q_hbm.1, bf16[256,1024]{1,0:T(8,128)(2,1)} %k_hbm.1, bf16[256,1024]{1,0:T(8,128)(2,1)} %v_hbm.1), custom_call_target="tpu_custom_call" | custom-call | tf_op jit(solution)/shard_map/pallas_call | solution.py:346
  24.6 0.8 %copy.5 = bf16[256,1024]{1,0:T(8,128)(2,1)} copy(bf16[256,1024]{1,0:T(8,128)(2,1)S(1)} %shard_map.37) | data formatting | bytes 1048576

commit v4 on v3

--- a/solution.py
+++ b/solution.py
@@ -12,9 +12,9 @@
 PAIRS = 8
 HALF = PAIRS // 2
 CHIPS = 8
-OWNED = (0, 1)
+OWNED = 2
 GREETED = (5, 4, 6, 3, 7, 2, 1, 0)
-ROWS = 64 // len(OWNED)
+ROWS = 64 // OWNED
 STATE = HALF * HEAD_DIM
 QUAD = 2 * PAIR
 BF16 = jnp.bfloat16
@@ -35,24 +35,29 @@
     tokens = q.shape[0]
     row_half = tokens // 2
     members = nx * CHIPS
-    owners = nx * len(OWNED)
+    owners = nx * OWNED
     wide = lax.axis_index("wide")
     z = lax.axis_index("chain")
     chip = wide // 2
     core = lax.rem(wide, 2)
     mate = {"wide": 2 * chip + 1 - core}
     x, y = chip // CHIPS, lax.rem(chip, CHIPS)
-    place = sum(jnp.where(y == there, i, 0) for i, there in enumerate(OWNED))
-    owns = functools.reduce(jnp.logical_or, [y == there for there in OWNED])
-    owner = x * len(OWNED) + place
-    near = sorted(range(nx), key=lambda d: min(d, nx - d))
-    far = near[::-1]
+    def shift(x_there, z_there):
+        return jnp.where((x_there == 0) & (z_there == 0), 1, 0)
+
+    offset = shift(x, z)
+    owns = (y >= offset) & (y < offset + OWNED)
+    owner = x * OWNED + y - offset
+    far = sorted(range(nx), key=lambda d: -min(d, nx - d))
 
     def plane_id(chip):
         return {"wide": 2 * chip + core}
 
+    def z_chip(i):
+        return chip - offset + shift(x, i)
+
     def z_id(i):
-        return {"chain": i}
+        return {"wide": 2 * z_chip(i) + core, "chain": i}
 
     def to_plane(columns, across, act):
         for there in columns:
@@ -63,10 +68,14 @@
                 else:
                     pl.when(there != y)(functools.partial(act, chip_there))
 
-    def owner_of(chip):
-        column = lax.rem(chip, CHIPS)
-        place = sum(jnp.where(column == there, i, 0) for i, there in enumerate(OWNED))
-        return chip // CHIPS * len(OWNED) + place
+    def to_owners(act):
+        for i in range(OWNED):
+            for d in far:
+                x_there = lax.rem(x + d, nx)
+                chip_there = x_there * CHIPS + i + shift(x_there, z)
+                pl.when(chip_there != chip)(
+                    functools.partial(act, chip_there, x_there * OWNED + i)
+                )
 
     loads = []
     for c in range(4):
@@ -99,7 +108,7 @@
         to_plane(GREETED, far, greet)
 
         def greet_later(i, _):
-            greet(chip, i)
+            greet(z_chip(i), i)
             return 0
 
         lax.fori_loop(z + 1, nz, greet_later, 0)
@@ -165,13 +174,13 @@
     def _():
         pl.semaphore_wait(all_here, 1)
 
-    def send_piece(there):
+    def send_piece(there, owner_there):
         pltpu.make_async_remote_copy(
-            src_ref=s_out.at[owner_of(there)], dst_ref=s_in.at[chip], send_sem=s_send, recv_sem=s_recv,
+            src_ref=s_out.at[owner_there], dst_ref=s_in.at[chip], send_sem=s_send, recv_sem=s_recv,
             device_id=plane_id(there), device_id_type=MESH,
         ).start()
 
-    to_plane(OWNED, far, send_piece)
+    to_owners(send_piece)
 
     @pl.when(owns)
     def _():
@@ -243,6 +252,8 @@
         pltpu.make_async_copy(z_in.at[i], z_in.at[i], z_recv.at[i]).wait()
         return acc + z_in[i]
 
+    soon = jnp.where(z == 0, nz // 2, nz)
+
     def z_done(i, _):
         pltpu.make_async_copy(z_out, z_out, z_send.at[i]).wait()
         return 0
@@ -263,13 +274,15 @@
         for i in range(1, members):
             plane = plane + s_in[i].astype(F32)
         z_out[...] = plane
-        lax.fori_loop(z + 1, nz, z_start, 0)
+        lax.fori_loop(z + 1, soon, z_start, 0)
         run = lax.fori_loop(0, z, z_take, jnp.zeros((ROWS, PAIR), F32))
         for i in range(members):
             p_out[i] = run.astype(BF16)
             if i + 1 < members:
                 run = run + s_in[i].astype(F32)
-        to_plane(range(CHIPS), far, send_back)
+        to_plane(range(CHIPS // 2), far, send_back)
+        lax.fori_loop(soon, nz, z_start, 0)
+        to_plane(range(CHIPS // 2, CHIPS), far, send_back)
         p_in[owner] = p_out[chip]
         wait_for(s_out, owners - 1, s_send)
         lax.fori_loop(z + 1, nz, z_done, 0)
@@ -336,7 +349,7 @@
 def solution(mesh):
     nx = mesh.shape["wide"] // (2 * CHIPS)
     nz = mesh.shape["chain"]
-    members, owners = nx * CHIPS, nx * len(OWNED)
+    members, owners = nx * CHIPS, nx * OWNED
 
     def per_device(queries, keys, values):
         tokens, width = queries.shape

time: 25.6 us -> 24.7 us (0.965)
  the two profiles are of different devices: /device:TPU:121 before, /device:TPU:481 now
where the time goes in v4:
time: 24.7 us; the launch traced here: 24.6 us
  Pallas kernels  23.7 us (96%)
  local copies, waits for them, and re-layouts  0.8 us (3%)
    pallas_call x1, Pallas kernels, per_device(): pl.pallas_call(functools.partial(attend_kernel, nx, nz), out_shape=jax.Sh...  23.7 us
    unnamed x1, local copies, waits for them, and re-layouts  0.8 us

profile of v4, /device:TPU:481, one launch (start us, length us, event | category | flops | bytes accessed | tf_op | source)
XLA Modules:
  0.0 24.6 jit_solution(3214332137227842883)
XLA Ops:
  0.0 23.7 %shard_map.37 = bf16[256,1024]{1,0:T(8,128)(2,1)S(1)} custom-call(bf16[256,1024]{1,0:T(8,128)(2,1)} %q_hbm.1, bf16[256,1024]{1,0:T(8,128)(2,1)} %k_hbm.1, bf16[256,1024]{1,0:T(8,128)(2,1)} %v_hbm.1), custom_call_target="tpu_custom_call" | custom-call | tf_op jit(solution)/shard_map/pallas_call | solution.py:359
  23.8 0.8 %copy.5 = bf16[256,1024]{1,0:T(8,128)(2,1)} copy(bf16[256,1024]{1,0:T(8,128)(2,1)S(1)} %shard_map.37) | data formatting | bytes 1048576

commit v5 on v4

--- a/solution.py
+++ b/solution.py
@@ -29,7 +29,7 @@
 def attend_kernel(
     nx, nz, q_hbm, k_hbm, v_hbm, o_ref,
     q, k, v, intra, given, mine, theirs, first, s_out, s_in, z_out, z_in, p_out, p_in, p_other,
-    in_sem, mate_send, mate_recv, s_send, s_recv, z_send, z_recv, p_send, p_recv, f_send, f_recv,
+    in_sem, swap_send, swap_recv, mate_send, mate_recv, s_send, s_recv, z_send, z_recv, p_send, p_recv, f_send, f_recv,
     mate_here, all_here, z_ready,
 ):
     tokens = q.shape[0]
@@ -129,23 +129,26 @@
         both = dot(k[:, cols], v[:, cols], ((0,), (0,)))
         return jnp.where(low, both[:HEAD_DIM], both[HEAD_DIM:])
 
-    def half_state(half, first_load, out):
+    def half_state(half, first_load, out, then=None):
         for j in range(HALF):
             if j % 2 == 0:
                 for load in loads[first_load + j // 2]:
                     load.wait()
             out[j * HEAD_DIM : (j + 1) * HEAD_DIM] = pair_state(half, j)
-
-    half_state(1 - core, 0, given)
-
-    swap = pltpu.make_async_remote_copy(
-        src_ref=given, dst_ref=theirs, send_sem=mate_send.at[0],
-        recv_sem=mate_recv.at[0], device_id=mate, device_id_type=MESH,
-    )
-    swap.start()
+            if j % 2 == 1 and then is not None:
+                then(j // 2)
+
+    def swap(part):
+        rows = pl.ds(part * 2 * HEAD_DIM, 2 * HEAD_DIM)
+        return pltpu.make_async_remote_copy(
+            src_ref=given.at[rows], dst_ref=theirs.at[rows], send_sem=swap_send.at[part],
+            recv_sem=swap_recv.at[part], device_id=mate, device_id_type=MESH,
+        )
+
+    half_state(1 - core, 0, given, lambda part: swap(part).start())
     half_state(core, 2, mine)
     extra = pltpu.make_async_remote_copy(
-        src_ref=mine, dst_ref=first, send_sem=mate_send.at[1], recv_sem=mate_recv.at[1],
+        src_ref=mine, dst_ref=first, send_sem=mate_send, recv_sem=mate_recv,
         device_id=mate, device_id_type=MESH,
     )
 
@@ -153,8 +156,9 @@
     def _():
         extra.start()
 
-    swap.wait_recv()
     for i in range(owners):
+        if i % (owners // 2) == 0:
+            swap(i // (owners // 2)).wait_recv()
         rows = slice(i * ROWS, (i + 1) * ROWS)
         s_out[i] = (mine[rows] + theirs[rows]).astype(BF16)
 
@@ -291,7 +295,8 @@
     def _():
         wait_for(s_out, owners, s_send)
 
-    swap.wait_send()
+    for part in range(2):
+        swap(part).wait_send()
     mean = jnp.where(
         lax.broadcasted_iota(jnp.int32, (QUAD, QUAD), 0) // HEAD_DIM
         == lax.broadcasted_iota(jnp.int32, (QUAD, QUAD), 1) // HEAD_DIM,
@@ -382,6 +387,8 @@
                 dma((2,)),
                 dma,
                 dma,
+                dma,
+                dma,
                 dma((nz,)),
                 dma((nz,)),
                 dma,

time: 24.7 us -> 24.6 us (level)
  no operation moved by 1% of the time
where the time goes in v5:
time: 24.6 us; the launch traced here: 24.5 us
  Pallas kernels  23.7 us (96%)
  local copies, waits for them, and re-layouts  0.8 us (3%)
    pallas_call x1, Pallas kernels, per_device(): pl.pallas_call(functools.partial(attend_kernel, nx, nz), out_shape=jax.Sh...  23.7 us
    unnamed x1, local copies, waits for them, and re-layouts  0.8 us

profile of v5, /device:TPU:481, one launch (start us, length us, event | category | flops | bytes accessed | tf_op | source)
XLA Modules:
  0.0 24.5 jit_solution(13815868771618513219)
XLA Ops:
  0.0 23.7 %shard_map.37 = bf16[256,1024]{1,0:T(8,128)(2,1)S(1)} custom-call(bf16[256,1024]{1,0:T(8,128)(2,1)} %q_hbm.1, bf16[256,1024]{1,0:T(8,128)(2,1)} %k_hbm.1, bf16[256,1024]{1,0:T(8,128)(2,1)} %v_hbm.1), custom_call_target="tpu_custom_call" | custom-call | tf_op jit(solution)/shard_map/pallas_call | solution.py:364
  23.7 0.8 %copy.5 = bf16[256,1024]{1,0:T(8,128)(2,1)} copy(bf16[256,1024]{1,0:T(8,128)(2,1)S(1)} %shard_map.37) | data formatting | bytes 1048576

commit v6 on v5

--- a/solution.py
+++ b/solution.py
@@ -152,10 +152,6 @@
         device_id=mate, device_id_type=MESH,
     )
 
-    @pl.when(core == 0)
-    def _():
-        extra.start()
-
     for i in range(owners):
         if i % (owners // 2) == 0:
             swap(i // (owners // 2)).wait_recv()
@@ -185,6 +181,10 @@
         ).start()
 
     to_owners(send_piece)
+
+    @pl.when(core == 0)
+    def _():
+        extra.start()
 
     @pl.when(owns)
     def _():

time: 24.6 us -> 24.6 us (level)
  no operation moved by 1% of the time
where the time goes in v6:
time: 24.6 us; the launch traced here: 24.5 us
  Pallas kernels  23.7 us (96%)
  local copies, waits for them, and re-layouts  0.8 us (3%)
    pallas_call x1, Pallas kernels, per_device(): pl.pallas_call(functools.partial(attend_kernel, nx, nz), out_shape=jax.Sh...  23.7 us
    unnamed x1, local copies, waits for them, and re-layouts  0.8 us

profile of v6, /device:TPU:481, one launch (start us, length us, event | category | flops | bytes accessed | tf_op | source)
XLA Modules:
  0.0 24.5 jit_solution(10494377674434560222)
XLA Ops:
  0.0 23.7 %shard_map.37 = bf16[256,1024]{1,0:T(8,128)(2,1)S(1)} custom-call(bf16[256,1024]{1,0:T(8,128)(2,1)} %q_hbm.1, bf16[256,1024]{1,0:T(8,128)(2,1)} %k_hbm.1, bf16[256,1024]{1,0:T(8,128)(2,1)} %v_hbm.1), custom_call_target="tpu_custom_call" | custom-call | tf_op jit(solution)/shard_map/pallas_call | solution.py:364
  23.7 0.8 %copy.5 = bf16[256,1024]{1,0:T(8,128)(2,1)} copy(bf16[256,1024]{1,0:T(8,128)(2,1)S(1)} %shard_map.37) | data formatting | bytes 1048576

commit v7 on v6

--- a/solution.py
+++ b/solution.py
@@ -69,7 +69,7 @@
                     pl.when(there != y)(functools.partial(act, chip_there))
 
     def to_owners(act):
-        for i in range(OWNED):
+        for i in range(OWNED)[::-1]:
             for d in far:
                 x_there = lax.rem(x + d, nx)
                 chip_there = x_there * CHIPS + i + shift(x_there, z)
@@ -284,9 +284,8 @@
             p_out[i] = run.astype(BF16)
             if i + 1 < members:
                 run = run + s_in[i].astype(F32)
-        to_plane(range(CHIPS // 2), far, send_back)
+        to_plane(range(CHIPS), far, send_back)
         lax.fori_loop(soon, nz, z_start, 0)
-        to_plane(range(CHIPS // 2, CHIPS), far, send_back)
         p_in[owner] = p_out[chip]
         wait_for(s_out, owners - 1, s_send)
         lax.fori_loop(z + 1, nz, z_done, 0)

time: 24.6 us -> 24.3 us (0.988)
  the two profiles are of different devices: /device:TPU:481 before, /device:TPU:289 now
where the time goes in v7:
time: 24.3 us; the launch traced here: 24.2 us
  Pallas kernels  23.4 us (96%)
  local copies, waits for them, and re-layouts  0.8 us (3%)
    pallas_call x1, Pallas kernels, per_device(): pl.pallas_call(functools.partial(attend_kernel, nx, nz), out_shape=jax.Sh...  23.4 us
    unnamed x1, local copies, waits for them, and re-layouts  0.8 us

profile of v7, /device:TPU:289, one launch (start us, length us, event | category | flops | bytes accessed | tf_op | source)
XLA Modules:
  0.0 24.2 jit_solution(9971957957263254012)
XLA Ops:
  0.0 23.4 %shard_map.37 = bf16[256,1024]{1,0:T(8,128)(2,1)S(1)} custom-call(bf16[256,1024]{1,0:T(8,128)(2,1)} %q_hbm.1, bf16[256,1024]{1,0:T(8,128)(2,1)} %k_hbm.1, bf16[256,1024]{1,0:T(8,128)(2,1)} %v_hbm.1), custom_call_target="tpu_custom_call" | custom-call | tf_op jit(solution)/shard_map/pallas_call | solution.py:363
  23.4 0.8 %copy.5 = bf16[256,1024]{1,0:T(8,128)(2,1)} copy(bf16[256,1024]{1,0:T(8,128)(2,1)S(1)} %shard_map.37) | data formatting | bytes 1048576
